TPU v7x, 32 devices: a whole 2x2x4 slice. The times are simulated.
32 devices in a mesh: days: 2 (over x), chan: 16 (over z, y, core).
Axes of the slice: x: 2, y: 2, z: 4, core: 2. Of those that a mesh axis runs over, the one named last changes fastest.
Arguments:
- spectra: bfloat16 [8, 512, 2048], P('days', None, 'chan'), may hold values from -6 to 6
- sources: int32 [2], replicated, may hold values from 0 to 2047
- offsets: int32 [2048], P('chan'), may hold values from 0 to 4095
Outputs:
- slant: float32 [128, 2, 2, 256], P('chan')
All inputs are finite; a program needn't handle non-finite values.
Results may differ from a plain program's by a relative error of at most 0.0055.
Values may be sent and summed in bfloat16 or wider, within the bound.
A program may use at most 64 MiB of HBM per device.

v0:
```python
import math

import jax
import jax.numpy as jnp
from jax import lax
from jax.sharding import PartitionSpec as P

NSLOW = 128
NSRC = 2


def from_root(value, axis, source):
    kept = jnp.where(lax.axis_index(axis) == source, value, 0).astype(value.dtype)
    return lax.psum(kept, axis)


def angles(left_index, right_index, period):
    return (left_index * right_index % period).astype(jnp.float32) * (2.0 * math.pi / period)


def inverse_table(bins):
    lag_total = 2 * bins
    theta = angles(
        jnp.arange(lag_total, dtype=jnp.int32)[:, None],
        jnp.arange(bins, dtype=jnp.int32)[None, :],
        lag_total,
    )
    cosine = jnp.cos(theta)
    sine = jnp.sin(theta)
    upper = jnp.concatenate([cosine, -sine], 1)
    lower = jnp.concatenate([sine, cosine], 1)
    return (jnp.concatenate([upper, lower], 0) / math.sqrt(bins)).astype(jnp.bfloat16)


def forward_table(bins, lag_count):
    lag_total = 2 * bins
    theta = angles(
        jnp.arange(bins, dtype=jnp.int32)[:, None],
        jnp.arange(lag_count, dtype=jnp.int32)[None, :],
        lag_total,
    )
    return jnp.concatenate([jnp.cos(theta), -jnp.sin(theta)], 0) / math.sqrt(lag_total)


def slant_block(spec_re, spec_im, slowness, offsets, bins):
    freq = jnp.arange(bins, dtype=jnp.int32)
    phase = freq[None, :, None] * slowness[:, None, None] % 4096 * offsets[None, None, :] % 4096
    theta = phase.astype(jnp.float32) * (2.0 * math.pi / 4096)
    cosine = jnp.cos(theta)
    sine = jnp.sin(theta)
    highest = lax.Precision.HIGHEST
    real_part = jnp.einsum("sfc,kfc->ksf", spec_re, cosine, precision=highest) - jnp.einsum(
        "sfc,kfc->ksf", spec_im, sine, precision=highest
    )
    imag_part = jnp.einsum("sfc,kfc->ksf", spec_re, sine, precision=highest) + jnp.einsum(
        "sfc,kfc->ksf", spec_im, cosine, precision=highest
    )
    return jnp.stack([real_part, imag_part], 2)


def shards(spectra, sources, offsets):
    window_count = spectra.shape[0]
    bins = spectra.shape[1] // 2
    lag_total = 2 * bins
    channel_width = spectra.shape[2]
    chan_devices = lax.axis_size("chan")
    day_devices = lax.axis_size("days")
    collected = []
    for source_number in range(NSRC):
        holder = sources[source_number] // channel_width
        column = sources[source_number] - holder * channel_width
        single = lax.dynamic_slice_in_dim(spectra, column, 1, 2)[:, :, 0]
        collected.append(from_root(single, "chan", holder))
    source_spectra = jnp.stack(collected, 1)
    inverse = inverse_table(bins)
    window_block = math.gcd(window_count, 8)

    def accumulate(block_number, totals):
        channel_part = spectra.astype(jnp.float32)
        source_part = source_spectra.astype(jnp.float32)
        real_x = channel_part[:, None, :bins]
        imag_x = channel_part[:, None, bins:]
        real_s = source_part[:, :, :bins, None]
        imag_s = source_part[:, :, bins:, None]
        product = jnp.concatenate(
            [real_s * real_x + imag_s * imag_x, real_s * imag_x - imag_s * real_x], 2
        ).astype(jnp.bfloat16)
        analytic = jnp.einsum("lk,wskc->wslc", inverse, product, preferred_element_type=jnp.float32)
        correlation = analytic[:, :, :lag_total]
        hilbert = analytic[:, :, lag_total:]
        magnitude = jnp.maximum(jnp.sqrt(correlation * correlation + hilbert * hilbert), 0.5)
        return (
            totals[0] + jnp.sum(correlation, 0),
            totals[1] + jnp.sum(correlation / magnitude, 0),
            totals[2] + jnp.sum(hilbert / magnitude, 0),
        )

    empty = jnp.zeros((NSRC, lag_total, channel_width), jnp.float32)
    linear, phase_re, phase_im = lax.fori_loop(
        0, window_count // window_block, accumulate, (empty, empty, empty)
    )
    linear, phase_re, phase_im = lax.psum((linear, phase_re, phase_im), "days")
    all_windows = window_count * day_devices
    weighted = (
        linear
        / all_windows
        * ((phase_re * phase_re + phase_im * phase_im) / (all_windows * all_windows))
    )
    forward = forward_table(bins, lag_total)
    spectrum = jnp.einsum("kt,stc->skc", forward, weighted, precision=lax.Precision.HIGHEST)
    spec_re = spectrum[:, :bins]
    spec_im = spectrum[:, bins:]
    scaling = all_windows**1.5 / math.sqrt(channel_width * chan_devices)
    owned_rows = NSLOW // chan_devices
    slow_count = lax.axis_size("chan") * owned_rows
    group_size = math.gcd(slow_count, 16)
    slowness = jnp.arange(slow_count, dtype=jnp.int32)

    def one_group(group_slowness):
        return slant_block(spec_re, spec_im, group_slowness, offsets, bins)

    pieces = lax.map(one_group, slowness.reshape(slow_count // group_size, group_size))
    return lax.psum_scatter(
        pieces.reshape(slow_count, NSRC, 2, bins) * scaling, "chan", scatter_dimension=0, tiled=True
    )


def solution(mesh):
    placed = (P("days", None, "chan"), P(), P("chan"))
    return jax.shard_map(
        shards, mesh=mesh, in_specs=placed, out_specs=P("chan", None, None, None), check_vma=False
    )
```

profile of v0, /device:TPU:0, one launch (start us, length us, event | category | flops | bytes accessed | tf_op | source)
XLA Modules:
  0.0 613.2 jit_solution(4432744480014857707)
XLA Ops:
  6.5 1.4 fusion.80
  14.2 2.9 fusion.67
  17.1 2.7 fusion.69
  19.8 0.4 constant_dynamic-slice_fusion.2
  20.2 0.2 copy.34
  20.4 0.2 copy.35
  20.7 35.5 %all-reduce.2 = (bf16[4,1,512]{2,0,1:T(4,128)(2,1)S(1)}, bf16[4,1,512]{2,0,1:T(4,128)(2,1)S(1)}) all-reduce(bf16[4,1,512]{2,0,1:T(4,128)(2,1)S(1)} %get-tuple-element.155, bf16[4,1,512]{2,0,1:T(4,128)(2,1)S(1)} %get-tuple-element.156), channel_id=1, replica_groups=mesh['days'=2,'chan'=16] {'chan'}, use_global_device_ids=true, to_apply=%region_1.2 | all-reduce | flops 4096 | bytes 16384 | tf_op jit(solution)/shard_map/psum | solution.py:14
  56.2 0.2 copy.27
  56.4 0.2 copy.29
  56.6 0.3 add_convert_fusion
  56.9 0.3 copy-done.1
  57.3 0.2 copy-done.2
  57.4 1.3 convolution_bitcast_fusion
  58.7 2.3 slice_reduce_fusion
  61.0 0.2 all-reduce.6.cloned.1.call-start
  61.3 2.1 sine_negate_fusion
  63.3 46.7 %all-reduce.8.cloned.1.call-done = (f32[2,512,128]{1,2,0:T(8,128)}, f32[2,512,128]{1,2,0:T(8,128)}, f32[2,512,128]{1,2,0:T(8,128)}) async-done(((f32[2,512,128]{1,2,0:T(8,128)}, f32[2,512,128]{1,2,0:T(8,128)}, f32[2,512,128]{1,2,0:T(8,128)}), (f32[2,512,128]{1,2,0:T(8,128)}, f32[2,512,128]{1,2,0:T(8,128)}, f32[2,512,128]{1,2,0:T(8,128)})) %all-reduce.8.cloned.1.call-update) | async-done | bytes 1572880 | tf_op jit(solution)/shard_map/psum | solution.py:102
  110.0 2.5 convolution_bitcast_fusion.1
  112.6 0.1 copy.30
  112.8 0.1 copy.31
  112.9 399.9 %while.8 = (s32[]{:T(128)}, f32[8,16,2,2,256]{4,1,3,2,0:T(8,128)S(1)}, s32[8,16]{1,0:T(8,128)S(1)}, s32[128]{0:T(128)S(1)}, f32[2,256,128]{2,0,1:T(2,128)S(1)}, /*index=5*/f32[2,256,128]{2,0,1:T(2,128)S(1)}, s32[]{:T(128)}) while((s32[]{:T(128)}, f32[8,16,2,2,256]{4,1,3,2,0:T(8,128)S(1)}, s32[8,16]{1,0:T(8,128)S(1)}, s32[128]{0:T(128)S(1)}, ...), condition=%wide.region_9.10_spmd, body=%wide.region_8.9_spmd.sunk | while | flops 79773696 | bytes 1591573 | solution.py:122
  113.0 12.4 %fusion.108 = f32[256,16,2]{1,2,0:T(2,128)S(1)} fusion(f32[2,256,128]{2,0,1:T(2,128)S(1)} %get-tuple-element.216, s32[128]{0:T(128)S(1)} %get-tuple-element.215, s32[16,256]{0,1:T(8,128)S(1)} %add_select_fusion.5), kind=kOutput, calls=%fused_computation.14.clone.1 | convolution fusion | flops 19922944 | bytes 311808 | tf_op jit(solution)/shard_map/while/body/eval_jaxpr/sfc,kfc->ksf/dot_general | solution.py:52
  125.5 12.4 %fusion.109 = f32[16,2,1,256]{0,1,3,2:T(2,128)S(1)} fusion(f32[256,16,2]{1,2,0:T(2,128)S(1)} %fusion.108, f32[2,256,128]{2,0,1:T(2,128)S(1)} %get-tuple-element.217, s32[128]{0:T(128)S(1)} %get-tuple-element.215, s32[16,256]{0,1:T(8,128)S(1)} %add_select_fusion.5), kind=kOutput, calls=%fused_computation.11.clone.1 | convolution fusion | flops 19931136 | bytes 344576 | tf_op jit(solution)/shard_map/while/body/eval_jaxpr/sfc,kfc->ksf/dot_general | solution.py:52
  137.9 0.1 copy.39
  138.0 12.4 %fusion.106 = f32[256,16,2]{1,2,0:T(2,128)S(1)} fusion(f32[2,256,128]{2,0,1:T(2,128)S(1)} %get-tuple-element.216, s32[128]{0:T(128)S(1)} %get-tuple-element.215, s32[16,256]{0,1:T(8,128)S(1)} %add_select_fusion.5), kind=kOutput, calls=%fused_computation.15.clone.1 | convolution fusion | flops 19922944 | bytes 311808 | tf_op jit(solution)/shard_map/while/body/eval_jaxpr/sfc,kfc->ksf/dot_general | solution.py:55
  150.4 12.4 %fusion.107 = f32[16,2,1,256]{0,1,3,2:T(2,128)S(1)} fusion(f32[256,16,2]{1,2,0:T(2,128)S(1)} %fusion.106, f32[2,256,128]{2,0,1:T(2,128)S(1)} %get-tuple-element.217, s32[128]{0:T(128)S(1)} %get-tuple-element.215, s32[16,256]{0,1:T(8,128)S(1)} %add_select_fusion.5), kind=kOutput, calls=%fused_computation.9.clone.1 | convolution fusion | flops 19931136 | bytes 344576 | tf_op jit(solution)/shard_map/while/body/eval_jaxpr/sfc,kfc->ksf/dot_general | solution.py:55
  162.8 0.1 copy.38
  163.0 12.4 %fusion.108 = f32[256,16,2]{1,2,0:T(2,128)S(1)} fusion(f32[2,256,128]{2,0,1:T(2,128)S(1)} %get-tuple-element.216, s32[128]{0:T(128)S(1)} %get-tuple-element.215, s32[16,256]{0,1:T(8,128)S(1)} %add_select_fusion.5), kind=kOutput, calls=%fused_computation.14.clone.1 | convolution fusion | flops 19922944 | bytes 311808 | tf_op jit(solution)/shard_map/while/body/eval_jaxpr/sfc,kfc->ksf/dot_general | solution.py:52
  175.4 12.4 %fusion.109 = f32[16,2,1,256]{0,1,3,2:T(2,128)S(1)} fusion(f32[256,16,2]{1,2,0:T(2,128)S(1)} %fusion.108, f32[2,256,128]{2,0,1:T(2,128)S(1)} %get-tuple-element.217, s32[128]{0:T(128)S(1)} %get-tuple-element.215, s32[16,256]{0,1:T(8,128)S(1)} %add_select_fusion.5), kind=kOutput, calls=%fused_computation.11.clone.1 | convolution fusion | flops 19931136 | bytes 344576 | tf_op jit(solution)/shard_map/while/body/eval_jaxpr/sfc,kfc->ksf/dot_general | solution.py:52
  188.0 12.4 %fusion.106 = f32[256,16,2]{1,2,0:T(2,128)S(1)} fusion(f32[2,256,128]{2,0,1:T(2,128)S(1)} %get-tuple-element.216, s32[128]{0:T(128)S(1)} %get-tuple-element.215, s32[16,256]{0,1:T(8,128)S(1)} %add_select_fusion.5), kind=kOutput, calls=%fused_computation.15.clone.1 | convolution fusion | flops 19922944 | bytes 311808 | tf_op jit(solution)/shard_map/while/body/eval_jaxpr/sfc,kfc->ksf/dot_general | solution.py:55
  200.3 12.4 %fusion.107 = f32[16,2,1,256]{0,1,3,2:T(2,128)S(1)} fusion(f32[256,16,2]{1,2,0:T(2,128)S(1)} %fusion.106, f32[2,256,128]{2,0,1:T(2,128)S(1)} %get-tuple-element.217, s32[128]{0:T(128)S(1)} %get-tuple-element.215, s32[16,256]{0,1:T(8,128)S(1)} %add_select_fusion.5), kind=kOutput, calls=%fused_computation.9.clone.1 | convolution fusion | flops 19931136 | bytes 344576 | tf_op jit(solution)/shard_map/while/body/eval_jaxpr/sfc,kfc->ksf/dot_general | solution.py:55
  212.8 0.1 copy.38
  213.0 12.4 %fusion.108 = f32[256,16,2]{1,2,0:T(2,128)S(1)} fusion(f32[2,256,128]{2,0,1:T(2,128)S(1)} %get-tuple-element.216, s32[128]{0:T(128)S(1)} %get-tuple-element.215, s32[16,256]{0,1:T(8,128)S(1)} %add_select_fusion.5), kind=kOutput, calls=%fused_computation.14.clone.1 | convolution fusion | flops 19922944 | bytes 311808 | tf_op jit(solution)/shard_map/while/body/eval_jaxpr/sfc,kfc->ksf/dot_general | solution.py:52
  225.4 12.4 %fusion.109 = f32[16,2,1,256]{0,1,3,2:T(2,128)S(1)} fusion(f32[256,16,2]{1,2,0:T(2,128)S(1)} %fusion.108, f32[2,256,128]{2,0,1:T(2,128)S(1)} %get-tuple-element.217, s32[128]{0:T(128)S(1)} %get-tuple-element.215, s32[16,256]{0,1:T(8,128)S(1)} %add_select_fusion.5), kind=kOutput, calls=%fused_computation.11.clone.1 | convolution fusion | flops 19931136 | bytes 344576 | tf_op jit(solution)/shard_map/while/body/eval_jaxpr/sfc,kfc->ksf/dot_general | solution.py:52
  237.8 0.1 copy.39
  237.9 12.4 %fusion.106 = f32[256,16,2]{1,2,0:T(2,128)S(1)} fusion(f32[2,256,128]{2,0,1:T(2,128)S(1)} %get-tuple-element.216, s32[128]{0:T(128)S(1)} %get-tuple-element.215, s32[16,256]{0,1:T(8,128)S(1)} %add_select_fusion.5), kind=kOutput, calls=%fused_computation.15.clone.1 | convolution fusion | flops 19922944 | bytes 311808 | tf_op jit(solution)/shard_map/while/body/eval_jaxpr/sfc,kfc->ksf/dot_general | solution.py:55
  250.3 12.4 %fusion.107 = f32[16,2,1,256]{0,1,3,2:T(2,128)S(1)} fusion(f32[256,16,2]{1,2,0:T(2,128)S(1)} %fusion.106, f32[2,256,128]{2,0,1:T(2,128)S(1)} %get-tuple-element.217, s32[128]{0:T(128)S(1)} %get-tuple-element.215, s32[16,256]{0,1:T(8,128)S(1)} %add_select_fusion.5), kind=kOutput, calls=%fused_computation.9.clone.1 | convolution fusion | flops 19931136 | bytes 344576 | tf_op jit(solution)/shard_map/while/body/eval_jaxpr/sfc,kfc->ksf/dot_general | solution.py:55
  263.0 12.4 %fusion.108 = f32[256,16,2]{1,2,0:T(2,128)S(1)} fusion(f32[2,256,128]{2,0,1:T(2,128)S(1)} %get-tuple-element.216, s32[128]{0:T(128)S(1)} %get-tuple-element.215, s32[16,256]{0,1:T(8,128)S(1)} %add_select_fusion.5), kind=kOutput, calls=%fused_computation.14.clone.1 | convolution fusion | flops 19922944 | bytes 311808 | tf_op jit(solution)/shard_map/while/body/eval_jaxpr/sfc,kfc->ksf/dot_general | solution.py:52
  275.4 12.4 %fusion.109 = f32[16,2,1,256]{0,1,3,2:T(2,128)S(1)} fusion(f32[256,16,2]{1,2,0:T(2,128)S(1)} %fusion.108, f32[2,256,128]{2,0,1:T(2,128)S(1)} %get-tuple-element.217, s32[128]{0:T(128)S(1)} %get-tuple-element.215, s32[16,256]{0,1:T(8,128)S(1)} %add_select_fusion.5), kind=kOutput, calls=%fused_computation.11.clone.1 | convolution fusion | flops 19931136 | bytes 344576 | tf_op jit(solution)/shard_map/while/body/eval_jaxpr/sfc,kfc->ksf/dot_general | solution.py:52
  287.9 12.4 %fusion.106 = f32[256,16,2]{1,2,0:T(2,128)S(1)} fusion(f32[2,256,128]{2,0,1:T(2,128)S(1)} %get-tuple-element.216, s32[128]{0:T(128)S(1)} %get-tuple-element.215, s32[16,256]{0,1:T(8,128)S(1)} %add_select_fusion.5), kind=kOutput, calls=%fused_computation.15.clone.1 | convolution fusion | flops 19922944 | bytes 311808 | tf_op jit(solution)/shard_map/while/body/eval_jaxpr/sfc,kfc->ksf/dot_general | solution.py:55
  300.3 12.4 %fusion.107 = f32[16,2,1,256]{0,1,3,2:T(2,128)S(1)} fusion(f32[256,16,2]{1,2,0:T(2,128)S(1)} %fusion.106, f32[2,256,128]{2,0,1:T(2,128)S(1)} %get-tuple-element.217, s32[128]{0:T(128)S(1)} %get-tuple-element.215, s32[16,256]{0,1:T(8,128)S(1)} %add_select_fusion.5), kind=kOutput, calls=%fused_computation.9.clone.1 | convolution fusion | flops 19931136 | bytes 344576 | tf_op jit(solution)/shard_map/while/body/eval_jaxpr/sfc,kfc->ksf/dot_general | solution.py:55
  312.7 0.1 copy.38
  313.0 12.4 %fusion.108 = f32[256,16,2]{1,2,0:T(2,128)S(1)} fusion(f32[2,256,128]{2,0,1:T(2,128)S(1)} %get-tuple-element.216, s32[128]{0:T(128)S(1)} %get-tuple-element.215, s32[16,256]{0,1:T(8,128)S(1)} %add_select_fusion.5), kind=kOutput, calls=%fused_computation.14.clone.1 | convolution fusion | flops 19922944 | bytes 311808 | tf_op jit(solution)/shard_map/while/body/eval_jaxpr/sfc,kfc->ksf/dot_general | solution.py:52
  325.4 12.4 %fusion.109 = f32[16,2,1,256]{0,1,3,2:T(2,128)S(1)} fusion(f32[256,16,2]{1,2,0:T(2,128)S(1)} %fusion.108, f32[2,256,128]{2,0,1:T(2,128)S(1)} %get-tuple-element.217, s32[128]{0:T(128)S(1)} %get-tuple-element.215, s32[16,256]{0,1:T(8,128)S(1)} %add_select_fusion.5), kind=kOutput, calls=%fused_computation.11.clone.1 | convolution fusion | flops 19931136 | bytes 344576 | tf_op jit(solution)/shard_map/while/body/eval_jaxpr/sfc,kfc->ksf/dot_general | solution.py:52
  337.8 0.1 copy.39
  337.9 12.4 %fusion.106 = f32[256,16,2]{1,2,0:T(2,128)S(1)} fusion(f32[2,256,128]{2,0,1:T(2,128)S(1)} %get-tuple-element.216, s32[128]{0:T(128)S(1)} %get-tuple-element.215, s32[16,256]{0,1:T(8,128)S(1)} %add_select_fusion.5), kind=kOutput, calls=%fused_computation.15.clone.1 | convolution fusion | flops 19922944 | bytes 311808 | tf_op jit(solution)/shard_map/while/body/eval_jaxpr/sfc,kfc->ksf/dot_general | solution.py:55
  350.3 12.4 %fusion.107 = f32[16,2,1,256]{0,1,3,2:T(2,128)S(1)} fusion(f32[256,16,2]{1,2,0:T(2,128)S(1)} %fusion.106, f32[2,256,128]{2,0,1:T(2,128)S(1)} %get-tuple-element.217, s32[128]{0:T(128)S(1)} %get-tuple-element.215, s32[16,256]{0,1:T(8,128)S(1)} %add_select_fusion.5), kind=kOutput, calls=%fused_computation.9.clone.1 | convolution fusion | flops 19931136 | bytes 344576 | tf_op jit(solution)/shard_map/while/body/eval_jaxpr/sfc,kfc->ksf/dot_general | solution.py:55
  363.0 12.4 %fusion.108 = f32[256,16,2]{1,2,0:T(2,128)S(1)} fusion(f32[2,256,128]{2,0,1:T(2,128)S(1)} %get-tuple-element.216, s32[128]{0:T(128)S(1)} %get-tuple-element.215, s32[16,256]{0,1:T(8,128)S(1)} %add_select_fusion.5), kind=kOutput, calls=%fused_computation.14.clone.1 | convolution fusion | flops 19922944 | bytes 311808 | tf_op jit(solution)/shard_map/while/body/eval_jaxpr/sfc,kfc->ksf/dot_general | solution.py:52
  375.4 12.4 %fusion.109 = f32[16,2,1,256]{0,1,3,2:T(2,128)S(1)} fusion(f32[256,16,2]{1,2,0:T(2,128)S(1)} %fusion.108, f32[2,256,128]{2,0,1:T(2,128)S(1)} %get-tuple-element.217, s32[128]{0:T(128)S(1)} %get-tuple-element.215, s32[16,256]{0,1:T(8,128)S(1)} %add_select_fusion.5), kind=kOutput, calls=%fused_computation.11.clone.1 | convolution fusion | flops 19931136 | bytes 344576 | tf_op jit(solution)/shard_map/while/body/eval_jaxpr/sfc,kfc->ksf/dot_general | solution.py:52
  387.9 12.4 %fusion.106 = f32[256,16,2]{1,2,0:T(2,128)S(1)} fusion(f32[2,256,128]{2,0,1:T(2,128)S(1)} %get-tuple-element.216, s32[128]{0:T(128)S(1)} %get-tuple-element.215, s32[16,256]{0,1:T(8,128)S(1)} %add_select_fusion.5), kind=kOutput, calls=%fused_computation.15.clone.1 | convolution fusion | flops 19922944 | bytes 311808 | tf_op jit(solution)/shard_map/while/body/eval_jaxpr/sfc,kfc->ksf/dot_general | solution.py:55
  400.3 12.4 %fusion.107 = f32[16,2,1,256]{0,1,3,2:T(2,128)S(1)} fusion(f32[256,16,2]{1,2,0:T(2,128)S(1)} %fusion.106, f32[2,256,128]{2,0,1:T(2,128)S(1)} %get-tuple-element.217, s32[128]{0:T(128)S(1)} %get-tuple-element.215, s32[16,256]{0,1:T(8,128)S(1)} %add_select_fusion.5), kind=kOutput, calls=%fused_computation.9.clone.1 | convolution fusion | flops 19931136 | bytes 344576 | tf_op jit(solution)/shard_map/while/body/eval_jaxpr/sfc,kfc->ksf/dot_general | solution.py:55
  412.9 12.4 %fusion.108 = f32[256,16,2]{1,2,0:T(2,128)S(1)} fusion(f32[2,256,128]{2,0,1:T(2,128)S(1)} %get-tuple-element.216, s32[128]{0:T(128)S(1)} %get-tuple-element.215, s32[16,256]{0,1:T(8,128)S(1)} %add_select_fusion.5), kind=kOutput, calls=%fused_computation.14.clone.1 | convolution fusion | flops 19922944 | bytes 311808 | tf_op jit(solution)/shard_map/while/body/eval_jaxpr/sfc,kfc->ksf/dot_general | solution.py:52
  425.4 12.4 %fusion.109 = f32[16,2,1,256]{0,1,3,2:T(2,128)S(1)} fusion(f32[256,16,2]{1,2,0:T(2,128)S(1)} %fusion.108, f32[2,256,128]{2,0,1:T(2,128)S(1)} %get-tuple-element.217, s32[128]{0:T(128)S(1)} %get-tuple-element.215, s32[16,256]{0,1:T(8,128)S(1)} %add_select_fusion.5), kind=kOutput, calls=%fused_computation.11.clone.1 | convolution fusion | flops 19931136 | bytes 344576 | tf_op jit(solution)/shard_map/while/body/eval_jaxpr/sfc,kfc->ksf/dot_general | solution.py:52
  437.8 0.1 copy.39
  437.9 12.4 %fusion.106 = f32[256,16,2]{1,2,0:T(2,128)S(1)} fusion(f32[2,256,128]{2,0,1:T(2,128)S(1)} %get-tuple-element.216, s32[128]{0:T(128)S(1)} %get-tuple-element.215, s32[16,256]{0,1:T(8,128)S(1)} %add_select_fusion.5), kind=kOutput, calls=%fused_computation.15.clone.1 | convolution fusion | flops 19922944 | bytes 311808 | tf_op jit(solution)/shard_map/while/body/eval_jaxpr/sfc,kfc->ksf/dot_general | solution.py:55
  450.3 12.4 %fusion.107 = f32[16,2,1,256]{0,1,3,2:T(2,128)S(1)} fusion(f32[256,16,2]{1,2,0:T(2,128)S(1)} %fusion.106, f32[2,256,128]{2,0,1:T(2,128)S(1)} %get-tuple-element.217, s32[128]{0:T(128)S(1)} %get-tuple-element.215, s32[16,256]{0,1:T(8,128)S(1)} %add_select_fusion.5), kind=kOutput, calls=%fused_computation.9.clone.1 | convolution fusion | flops 19931136 | bytes 344576 | tf_op jit(solution)/shard_map/while/body/eval_jaxpr/sfc,kfc->ksf/dot_general | solution.py:55
  462.9 12.4 %fusion.108 = f32[256,16,2]{1,2,0:T(2,128)S(1)} fusion(f32[2,256,128]{2,0,1:T(2,128)S(1)} %get-tuple-element.216, s32[128]{0:T(128)S(1)} %get-tuple-element.215, s32[16,256]{0,1:T(8,128)S(1)} %add_select_fusion.5), kind=kOutput, calls=%fused_computation.14.clone.1 | convolution fusion | flops 19922944 | bytes 311808 | tf_op jit(solution)/shard_map/while/body/eval_jaxpr/sfc,kfc->ksf/dot_general | solution.py:52
  475.3 12.4 %fusion.109 = f32[16,2,1,256]{0,1,3,2:T(2,128)S(1)} fusion(f32[256,16,2]{1,2,0:T(2,128)S(1)} %fusion.108, f32[2,256,128]{2,0,1:T(2,128)S(1)} %get-tuple-element.217, s32[128]{0:T(128)S(1)} %get-tuple-element.215, s32[16,256]{0,1:T(8,128)S(1)} %add_select_fusion.5), kind=kOutput, calls=%fused_computation.11.clone.1 | convolution fusion | flops 19931136 | bytes 344576 | tf_op jit(solution)/shard_map/while/body/eval_jaxpr/sfc,kfc->ksf/dot_general | solution.py:52
  487.9 12.4 %fusion.106 = f32[256,16,2]{1,2,0:T(2,128)S(1)} fusion(f32[2,256,128]{2,0,1:T(2,128)S(1)} %get-tuple-element.216, s32[128]{0:T(128)S(1)} %get-tuple-element.215, s32[16,256]{0,1:T(8,128)S(1)} %add_select_fusion.5), kind=kOutput, calls=%fused_computation.15.clone.1 | convolution fusion | flops 19922944 | bytes 311808 | tf_op jit(solution)/shard_map/while/body/eval_jaxpr/sfc,kfc->ksf/dot_general | solution.py:55
  500.2 12.4 %fusion.107 = f32[16,2,1,256]{0,1,3,2:T(2,128)S(1)} fusion(f32[256,16,2]{1,2,0:T(2,128)S(1)} %fusion.106, f32[2,256,128]{2,0,1:T(2,128)S(1)} %get-tuple-element.217, s32[128]{0:T(128)S(1)} %get-tuple-element.215, s32[16,256]{0,1:T(8,128)S(1)} %add_select_fusion.5), kind=kOutput, calls=%fused_computation.9.clone.1 | convolution fusion | flops 19931136 | bytes 344576 | tf_op jit(solution)/shard_map/while/body/eval_jaxpr/sfc,kfc->ksf/dot_general | solution.py:55
  512.9 1.2 copy.32
  514.1 0.6 dynamic-slice
  515.4 89.6 %all-reduce.6.cloned.1.call-done = f32[128,2,2,256]{3,2,1,0:T(2,128)} async-done(((f32[128,2,2,256]{3,2,1,0:T(2,128)}), f32[128,2,2,256]{3,2,1,0:T(2,128)}) %all-reduce.6.cloned.1.call-update) | async-done | bytes 524304
  605.0 1.4 constant_dynamic-slice_fusion
  (54 shorter events, 1.9 us)
Async XLA Ops:
  6.5 13.2 %copy-start = (bf16[4,512,128]{2,1,0:T(8,128)(2,1)S(1)}, bf16[4,512,128]{2,1,0:T(8,128)(2,1)}, u32[]{:S(2)}) copy-start(bf16[4,512,128]{2,1,0:T(8,128)(2,1)} %param.5) | copy-start | bytes 1572868
  6.5 103.5 %all-reduce.8.cloned.1.call-start = ((), (), s32[]{:S(2)}) async-start(), calls=%async_computation.1 | async-start | bytes 3145728 | tf_op jit(solution)/shard_map/psum | solution.py:102
  56.2 1.0 copy-start.1
  56.2 1.2 copy-start.2
  61.0 543.9 %all-reduce.6.cloned.1.call-start = ((), (), s32[]{:S(2)}) async-start(), calls=%async_computation | async-start | bytes 1048576
  110.0 2.9 copy-start.3
  512.8 1.3 copy-start.4
Sparse Core Ops, SparseCore 0:
  61.1 48.8 all-reduce.7
  514.2 90.6 all-reduce.5
where the time goes:
time: 614 us; the launch traced here: 613 us
  matrix products  401 us (65%)
  waiting for transfers between devices  136 us (22%)
  blocking collectives  35.5 us (6%)
  between operations  20.5 us (3%)
  other arithmetic  10.9 us (2%)
  local copies, waits for them, and re-layouts  8.37 us (1%)
    dot_general x8, matrix products, slant_block(): jnp.einsum('sfc,kfc->ksf', spec_im, cosine, precision=highest)  99.4 us
    dot_general x8, matrix products, slant_block(): jnp.einsum('sfc,kfc->ksf', spec_re, cosine, precision=highest)  99.3 us
    dot_general x8, matrix products, slant_block(): jnp.einsum('sfc,kfc->ksf', spec_im, sine, precision=highest)  99.3 us
    dot_general x8, matrix products, slant_block(): jnp.einsum('sfc,kfc->ksf', spec_re, sine, precision=highest)  99 us
    unnamed x3, waiting for transfers between devices  89.6 us
    psum x1, waiting for transfers between devices, shards(): linear, phase_re, phase_im = lax.psum((linear, phase_re, phase_im), 'days')  46.7 us
    psum x1, blocking collectives, from_root(): return lax.psum(kept, axis)  35.5 us
  transfers between devices with their start and end apart: 2, of which 2 were waited for; matrix products, arithmetic and copies ran while one was open for 0% of the time, Pallas kernels for 0%

commit v1 on v0

v1 whole, which is shorter than its diff:
```python
import functools
import math

import jax
import jax.numpy as jnp
import numpy as np
from jax import lax
from jax.experimental import pallas as pl
from jax.experimental.pallas import tpu as pltpu
from jax.sharding import PartitionSpec as P

NSLOW = 128
NSRC = 2
PERIOD = 4096
TILE = 8
LANES = 128
GROUP = 2


def tables(bins):
    lag_total = 2 * bins
    lag = np.arange(lag_total)[:, None]
    freq = np.arange(bins)[None, :]
    theta = (lag * freq % lag_total) * (2.0 * math.pi / lag_total)
    cosine, sine = np.cos(theta), np.sin(theta)
    inverse = np.concatenate(
        [np.concatenate([cosine, -sine], 1), np.concatenate([sine, cosine], 1)], 0
    ) / math.sqrt(bins)
    forward = np.concatenate([cosine, -sine], 1) / math.sqrt(lag_total)
    return (
        inverse.astype(np.float32).astype(jnp.bfloat16),
        forward.astype(np.float32).astype(jnp.bfloat16),
    )


def cos_sin(steps):
    quarter = PERIOD // 4
    place = steps & (PERIOD - 1)
    quadrant = (place + quarter // 2) // quarter
    x = (place - quadrant * quarter).astype(jnp.float32) * (2.0 * math.pi / PERIOD)
    y = x * x
    sine = x * (1.0 + y * (-1.0 / 6 + y * (1.0 / 120 - y * (1.0 / 5040))))
    cosine = 1.0 + y * (-0.5 + y * (1.0 / 24 + y * (-1.0 / 720 + y * (1.0 / 40320))))
    odd = (quadrant & 1) == 1
    first = jnp.where(odd, sine, cosine)
    second = jnp.where(odd, cosine, sine)
    first = jnp.where(((quadrant + 1) & 2) == 2, -first, first)
    second = jnp.where((quadrant & 2) == 2, -second, second)
    return first, second


def correlate(x_ref, s_ref, inverse_ref, forward_ref, analytic, weighted, spectrum, windows):
    count, depth, width = x_ref.shape
    bins, half = depth // 2, width // 2
    lags = depth
    wide = NSRC * width
    rows = lax.broadcasted_iota(jnp.int32, (s_ref.shape[1], wide), 0)
    lane = lax.broadcasted_iota(jnp.int32, (s_ref.shape[1], wide), 1)
    wanted = lane // width * 2 + lane % width // half
    for w in range(count):
        pick = (rows == w * (2 * NSRC) + wanted).astype(jnp.float32).astype(jnp.bfloat16)
        source = jnp.dot(s_ref[...], pick, preferred_element_type=jnp.float32)
        channel = x_ref[w].astype(jnp.float32)
        channel = jnp.concatenate([channel] * NSRC, 1)
        real_s, imag_s = source[:bins], source[bins:]
        real_x, imag_x = channel[:bins], channel[bins:]
        product = jnp.concatenate(
            [real_s * real_x + imag_s * imag_x, real_s * imag_x - imag_s * real_x], 0
        ).astype(jnp.bfloat16)
        analytic[w] = jnp.dot(inverse_ref[...], product, preferred_element_type=jnp.float32)

    block = 16

    def stack(step, carry):
        start = pl.multiple_of(step * block, block)
        linear = phase_re = phase_im = 0.0
        for w in range(count):
            corr = analytic[w, pl.ds(start, block)]
            hilb = analytic[w, pl.ds(lags + start, block)]
            over = jnp.minimum(lax.rsqrt(corr * corr + hilb * hilb), 2.0)
            linear = linear + corr
            phase_re = phase_re + corr * over
            phase_im = phase_im + hilb * over

        def fold(value):
            parts = []
            for s in range(NSRC):
                part = value[:, s * width : (s + 1) * width]
                parts.append(part + pltpu.roll(part, half, 1))
            side = lax.broadcasted_iota(jnp.int32, (block, width), 1) < half
            return jnp.where(side, parts[0], parts[1])

        linear, phase_re, phase_im = fold(linear), fold(phase_re), fold(phase_im)
        result = linear * (phase_re * phase_re + phase_im * phase_im) * (1.0 / windows**3)
        weighted[pl.ds(start, block)] = result.astype(jnp.bfloat16)
        return carry

    lax.fori_loop(0, lags // block, stack, 0)
    result = lax.dot_general(
        weighted[...], forward_ref[...], (((0,), (0,)), ((), ())), preferred_element_type=jnp.float32
    )
    for part in range(depth // LANES):
        spectrum[part] = result[:, part * LANES : (part + 1) * LANES]


def slant(offset_ref, spectrum, base, out_ref, half, bins, scaling):
    out_ref[...] = jnp.zeros_like(out_ref)
    steps = NSLOW // TILE
    low = lax.broadcasted_iota(jnp.int32, (TILE, LANES), 0)
    for part in range(bins // LANES):
        freq = lax.broadcasted_iota(jnp.int32, (TILE, LANES), 1) + part * LANES
        product = low * freq
        lanes = pl.ds(part * LANES, LANES)
        part_im = bins // LANES + part

        def group(number, carry):
            now, before, twice = [], [], []
            for member in range(GROUP):
                channel = number * GROUP + member
                offset = offset_ref[base + channel]
                jump_cos, jump_sin = cos_sin(freq * (offset * TILE))
                cosine, sine = cos_sin(product * offset)
                back_cos = cosine * jump_cos + sine * jump_sin
                back_sin = sine * jump_cos - cosine * jump_sin
                twice.append(2.0 * jump_cos)
                for s in range(NSRC):
                    row = pl.ds(s * half + channel, 1)
                    real = spectrum[part, row] * scaling
                    imag = spectrum[part_im, row] * scaling
                    now.append([real * cosine - imag * sine, real * sine + imag * cosine])
                    before.append([real * back_cos - imag * back_sin, real * back_sin + imag * back_cos])
            for step in range(steps):
                for s in range(NSRC):
                    for piece in range(2):
                        total = now[s][piece]
                        for member in range(1, GROUP):
                            total = total + now[member * NSRC + s][piece]
                        here = (s, piece, pl.ds(step * TILE, TILE), lanes)
                        out_ref[here] = out_ref[here] + total
                if step + 1 < steps:
                    for member in range(GROUP):
                        for s in range(NSRC):
                            at = member * NSRC + s
                            for piece in range(2):
                                later = twice[member] * now[at][piece] - before[at][piece]
                                before[at][piece] = now[at][piece]
                                now[at][piece] = later
            return carry

        lax.fori_loop(0, half // GROUP, group, 0)


def compute_kernel(windows, scaling, x_ref, s_ref, inverse_ref, forward_ref, offset_ref, out_ref, analytic, weighted, spectrum):
    half, bins = x_ref.shape[2] // 2, x_ref.shape[1] // 2
    correlate(x_ref, s_ref, inverse_ref, forward_ref, analytic, weighted, spectrum, windows)
    slant(offset_ref, spectrum, 0, out_ref, half, bins, scaling)


def shards(spectra, sources, offsets):
    count, depth, width = spectra.shape
    bins, half = depth // 2, width // 2
    day_devices, chan_devices = lax.axis_size("days"), lax.axis_size("chan")
    windows = count * day_devices
    me = lax.axis_index("days")
    swap = [(0, 1), (1, 0)]
    collected = []
    for number in range(NSRC):
        holder = sources[number] // width
        column = sources[number] - holder * width
        single = lax.dynamic_slice_in_dim(spectra, column, 1, 2)[:, :, 0]
        collected.append(jnp.where(lax.axis_index("chan") == holder, single, 0).astype(spectra.dtype))
    own = lax.psum(jnp.stack(collected, 1), "chan")
    other = lax.ppermute(own, "days", swap)
    source = jnp.stack([own, other], 2).transpose(3, 0, 1, 2).reshape(depth, count * NSRC * 2)
    kept = lax.dynamic_slice_in_dim(spectra, me * half, half, 2)
    sent = lax.dynamic_slice_in_dim(spectra, (1 - me) * half, half, 2)
    got = lax.ppermute(sent, "days", swap)
    paired = jnp.concatenate([kept, got], 2)
    inverse, forward = tables(bins)
    mine = lax.dynamic_slice_in_dim(offsets, me * half, half, 0)
    scaling = windows**1.5 / math.sqrt(width * chan_devices)
    vmem = pl.BlockSpec(memory_space=pltpu.VMEM)
    partial = pl.pallas_call(
        functools.partial(compute_kernel, windows, scaling),
        out_shape=jax.ShapeDtypeStruct((NSRC, 2, NSLOW, bins), jnp.float32),
        in_specs=[vmem] * 4 + [pl.BlockSpec(memory_space=pltpu.SMEM)],
        out_specs=vmem,
        scratch_shapes=[
            pltpu.VMEM((count, 2 * depth, NSRC * width), jnp.float32),
            pltpu.VMEM((depth, width), jnp.bfloat16),
            pltpu.VMEM((depth // LANES, NSRC * half, LANES), jnp.float32),
        ],
    )(paired, source, jnp.asarray(inverse), jnp.asarray(forward), mine)
    owned = lax.psum_scatter(partial.transpose(2, 0, 1, 3), "chan", scatter_dimension=0, tiled=True)
    return lax.psum(owned, "days")


def solution(mesh):
    placed = (P("days", None, "chan"), P(), P("chan"))
    return jax.shard_map(
        shards, mesh=mesh, in_specs=placed, out_specs=P("chan", None, None, None), check_vma=False
    )
```

time: 614 us -> 142 us (0.23)
  matrix products: 401 us -> 0 us
  waiting for transfers between devices: 136 us -> 55.1 us
  Pallas kernels: 0 us -> 14 us
  other arithmetic: 10.9 us -> 1.12 us
  blocking collectives: 35.5 us -> 42.7 us
    dot_general x34 -> x0, matrix products: 401 us -> none  [the longest x8 99.4 us: slant_block(): jnp.einsum('sfc,kfc->ksf', spec_im, cosine, precision=highest)]
    unnamed x3 -> x1, waiting for transfers between devices: 89.6 us -> 0.02 us
    reduce_scatter x0 -> x1, waiting for transfers between devices: none -> 52.9 us  [shards(): lax.psum_scatter(partial.transpose(2, 0, 1, 3), 'chan', scatter_dimension...]
    psum x1 -> x0, waiting for transfers between devices: 46.7 us -> none  [shards(): linear, phase_re, phase_im = lax.psum((linear, phase_re, phase_im), 'days')]
    pallas_call x0 -> x1, Pallas kernels: none -> 14 us  [shards(): pl.pallas_call(functools.partial(compute_kernel, windows, scaling), out_s...]
    psum x1 -> x2, blocking collectives: 35.5 us -> 42.7 us  [the longest x1 33.7 us: shards(): own = lax.psum(jnp.stack(collected, 1), 'chan')]
  transfers between devices with their start and end apart: 2 -> 3, of which waited for: 2 -> 2; matrix products, arithmetic and copies ran while one was open for 0% -> 2% of each run, Pallas kernels for 0% -> 0%
where the time goes in v1:
time: 142 us
  waiting for transfers between devices  55.1 us (39%)
  blocking collectives  42.7 us (30%)
  between operations  19.8 us (14%)
  Pallas kernels  14 us (10%)
  local copies, waits for them, and re-layouts  5.03 us (4%)
  starting transfers between devices  3.96 us (3%)
    reduce_scatter x1, waiting for transfers between devices, shards(): lax.psum_scatter(partial.transpose(2, 0, 1, 3), 'chan', scatter_dimension...  52.9 us
    psum x1, blocking collectives, shards(): own = lax.psum(jnp.stack(collected, 1), 'chan')  33.7 us
    pallas_call x1, Pallas kernels, shards(): pl.pallas_call(functools.partial(compute_kernel, windows, scaling), out_s...  14 us
    psum x1, blocking collectives, shards(): return lax.psum(owned, 'days')  8.96 us
    ppermute x1, starting transfers between devices, shards(): got = lax.ppermute(sent, 'days', swap)  3.03 us
  transfers between devices with their start and end apart: 3, of which 2 were waited for; matrix products, arithmetic and copies ran while one was open for 2% of the time, Pallas kernels for 0%

profile of v1, /device:TPU:0, one launch (start us, length us, event | category | flops | bytes accessed | tf_op | source)
XLA Modules:
  0.0 141.8 jit_solution(1115264818607667201)
XLA Ops:
  6.5 0.0 reduce-scatter.2.cloned.1.call-start
  6.5 0.0 copy-start
  6.5 1.6 %constant_dynamic-slice_fusion.3 = (bf16[4,512,64]{2,1,0:T(8,128)(2,1)S(1)}, bf16[4,512,64]{2,1,0:T(8,128)(2,1)S(1)}) fusion(bf16[4,512,128]{2,1,0:T(8,128)(2,1)} %param.5, s32[]{:T(128)S(6)} %select_n.55, s32[]{:T(128)S(6)} %select_n.56), kind=kLoop, calls=%fused_computation.8 | loop fusion | bytes 1048584 | tf_op jit(solution)/shard_map/dynamic_slice | solution.py:175
  8.2 0.0 copy-start.1
  8.2 3.0 %collective-permute-start = (bf16[4,512,64]{2,1,0:T(8,128)(2,1)S(1)}, bf16[4,512,64]{2,1,0:T(8,128)(2,1)S(1)}, u32[]{:S(2)}, u32[]{:S(2)}) collective-permute-start(bf16[4,512,64]{2,1,0:T(8,128)(2,1)S(1)} %get-tuple-element.8), channel_id=1, source_target_pairs={{0,16},{16,0},{1,17},{17,1},{2,18},{18,2},{3,19},{19,3},{4,20},{20... | collective-permute-start | bytes 786440 | tf_op jit(solution)/shard_map/ppermute | solution.py:177
  11.2 0.0 copy-done.1
  11.2 0.6 fusion
  18.1 0.0 copy-done
  18.1 0.4 constant_dynamic-slice_fusion.1
  18.5 0.2 copy.16
  18.7 0.2 copy.15
  19.0 0.0 copy-start.2
  19.0 33.7 %psum.14 = bf16[4,2,512]{2,0,1:T(4,128)(2,1)S(1)} all-reduce(bf16[4,2,512]{2,0,1:T(4,128)(2,1)S(1)} %pad_maximum_fusion.1), channel_id=1, replica_groups=mesh['days'=2,'chan'=16] {'chan'}, use_global_device_ids=true, to_apply=%region_0.1 | all-reduce | flops 4096 | bytes 16384 | tf_op jit(solution)/shard_map/psum | solution.py:172
  52.7 0.9 collective-permute-start.1
  53.7 0.0 copy-done.2
  53.7 0.6 dynamic_slice.19.offset_ref
  54.3 2.2 %collective-permute-done.1 = bf16[4,2,512]{2,0,1:T(4,128)(2,1)S(1)} collective-permute-done((bf16[4,2,512]{2,0,1:T(4,128)(2,1)S(1)}, bf16[4,2,512]{2,0,1:T(4,128)(2,1)S(1)}, u32[]{:S(2)}, u32[]{:S(2)}) %collective-permute-start.1) | collective-permute-done | bytes 8224 | tf_op jit(solution)/shard_map/ppermute | solution.py:173
  56.5 0.8 copy.13.s_ref
  57.3 0.0 collective-permute-done
  57.3 1.1 pad_maximum_fusion.x_ref
  58.4 14.0 %shard_map.55 = f32[2,2,128,256]{3,2,1,0:T(8,128)} custom-call(bf16[4,512,128]{2,1,0:T(8,128)(2,1)} %pad_maximum_fusion.x_ref, bf16[512,16]{1,0:T(8,128)(2,1)} %copy.13.s_ref, bf16[1024,512]{1,0:T(8,128)(2,1)} %constant.43.clone.inverse_ref, bf16[512,512]{1,0:T(8,128)(2,1)} %constant.44.clone.forward_ref, s32[64]{0:T(128)} %dynamic_slice.19.offset_ref), custom_call_target="tpu_custom_call" | custom-call | tf_op jit(solution)/shard_map/pallas_call | solution.py:183
  72.4 0.0 reduce-scatter.2.cloned.1.call-update
  72.4 52.9 %reduce-scatter.2.cloned.1.call-done = f32[8,2,2,256]{3,0,2,1:T(8,128)} async-done(((f32[128,2,2,256]{3,0,2,1:T(8,128)}), f32[8,2,2,256]{3,0,2,1:T(8,128)}) %reduce-scatter.2.cloned.1.call-update) | async-done | bytes 32784 | tf_op jit(solution)/shard_map/reduce_scatter | solution.py:194
  125.3 9.0 %psum.15 = f32[8,2,2,256]{3,0,2,1:T(8,128)S(1)} all-reduce(f32[8,2,2,256]{3,0,2,1:T(8,128)} %reduce-scatter.2.cloned.1.call-done), channel_id=1, replica_groups=mesh['days'=2,'chan'=16] {'days'}, use_global_device_ids=true, to_apply=%region_2.3 | all-reduce | flops 8192 | bytes 65536 | tf_op jit(solution)/shard_map/psum | solution.py:195
  134.3 0.6 copy.14
  (5 shorter events, 0.1 us)
Async XLA Ops:
  6.5 118.8 %reduce-scatter.2.cloned.1.call-start = ((), (), s32[]{:S(2)}) async-start(), calls=%async_computation.1 | async-start | bytes 557056 | tf_op jit(solution)/shard_map/reduce_scatter | solution.py:194
  6.5 11.6 %copy-start = (bf16[4,512,128]{2,1,0:T(8,128)(2,1)S(1)}, bf16[4,512,128]{2,1,0:T(8,128)(2,1)}, u32[]{:S(2)}) copy-start(bf16[4,512,128]{2,1,0:T(8,128)(2,1)} %param.5) | copy-start | bytes 1572868
  8.2 3.0 %copy-start.1 = (s32[2]{0:T(128)S(1)}, s32[2]{0:T(128)}, u32[]{:S(2)}) copy-start(s32[2]{0:T(128)} %param.6) | copy-start | bytes 28
  8.2 49.1 %collective-permute-start = (bf16[4,512,64]{2,1,0:T(8,128)(2,1)S(1)}, bf16[4,512,64]{2,1,0:T(8,128)(2,1)S(1)}, u32[]{:S(2)}, u32[]{:S(2)}) collective-permute-start(bf16[4,512,64]{2,1,0:T(8,128)(2,1)S(1)} %get-tuple-element.8), channel_id=1, source_target_pairs={{0,16},{16,0},{1,17},{17,1},{2,18},{18,2},{3,19},{19,3},{4,20},{20... | collective-permute-start | bytes 786440 | tf_op jit(solution)/shard_map/ppermute | solution.py:177
  19.0 34.7 %copy-start.2 = (s32[128]{0:T(128)S(1)}, s32[128]{0:T(128)}, u32[]{:S(2)}) copy-start(s32[128]{0:T(128)} %param.7) | copy-start | bytes 1540
  52.7 3.7 %collective-permute-start.1 = (bf16[4,2,512]{2,0,1:T(4,128)(2,1)S(1)}, bf16[4,2,512]{2,0,1:T(4,128)(2,1)S(1)}, u32[]{:S(2)}, u32[]{:S(2)}) collective-permute-start(bf16[4,2,512]{2,0,1:T(4,128)(2,1)S(1)} %psum.14), channel_id=1, source_target_pairs={{0,16},{16,0},{1,17},{17,1},{2,18},{18,2},{3,19},{19,3},{4,20},{20... | collective-permute-start | bytes 24584 | tf_op jit(solution)/shard_map/ppermute | solution.py:173
Sparse Core Ops, SparseCore 0:
  72.5 52.7 reduce-scatter.1

commit v2 on v1

v2 whole, which is shorter than its diff:
```python
import functools
import math

import jax
import jax.numpy as jnp
import numpy as np
from jax import lax
from jax.experimental import pallas as pl
from jax.experimental.pallas import tpu as pltpu
from jax.sharding import PartitionSpec as P

NSLOW = 128
NSRC = 2
PERIOD = 4096
TILE = 8
LANES = 128
GROUP = 2
NEAR = 4


def tables(bins):
    lag_total = 2 * bins
    lag = np.arange(lag_total)[:, None]
    freq = np.arange(bins)[None, :]
    theta = (lag * freq % lag_total) * (2.0 * math.pi / lag_total)
    cosine, sine = np.cos(theta), np.sin(theta)
    inverse = np.concatenate(
        [np.concatenate([cosine, -sine], 1), np.concatenate([sine, cosine], 1)], 0
    ) / math.sqrt(bins)
    forward = np.concatenate([cosine, -sine], 1) / math.sqrt(lag_total)
    return (
        inverse.astype(np.float32).astype(jnp.bfloat16),
        forward.astype(np.float32).astype(jnp.bfloat16),
    )


def cos_sin(steps):
    quarter = PERIOD // 4
    place = steps & (PERIOD - 1)
    quadrant = (place + quarter // 2) // quarter
    x = (place - quadrant * quarter).astype(jnp.float32) * (2.0 * math.pi / PERIOD)
    y = x * x
    sine = x * (1.0 + y * (-1.0 / 6 + y * (1.0 / 120 - y * (1.0 / 5040))))
    cosine = 1.0 + y * (-0.5 + y * (1.0 / 24 + y * (-1.0 / 720 + y * (1.0 / 40320))))
    odd = (quadrant & 1) == 1
    first = jnp.where(odd, sine, cosine)
    second = jnp.where(odd, cosine, sine)
    first = jnp.where(((quadrant + 1) & 2) == 2, -first, first)
    second = jnp.where((quadrant & 2) == 2, -second, second)
    return first, second


def exchange(source, target, send_sem, recv_sem, day, chan):
    return pltpu.make_async_remote_copy(
        src_ref=source,
        dst_ref=target,
        send_sem=send_sem,
        recv_sem=recv_sem,
        device_id={"days": day, "chan": chan},
        device_id_type=pl.DeviceIdType.MESH,
    )


def pack_halves(spectra_ref, kept, sent, day):
    count, depth, width = spectra_ref.shape
    half = width // 2
    left = lax.broadcasted_iota(jnp.int32, (depth, width), 1) < half
    upper = jnp.full((depth, width), day, jnp.int32) == 1
    for pair in range(count // 2):
        first = spectra_ref[2 * pair].astype(jnp.float32)
        second = spectra_ref[2 * pair + 1].astype(jnp.float32)
        lows = jnp.where(left, first, pltpu.roll(second, half, 1))
        highs = jnp.where(left, pltpu.roll(first, half, 1), second)
        kept[pair] = jnp.where(upper, highs, lows).astype(jnp.bfloat16)
        sent[pair] = jnp.where(upper, lows, highs).astype(jnp.bfloat16)


def source_columns(spectra_ref, sources_ref, chan):
    count, depth, width = spectra_ref.shape
    shape = (count * NSRC, width)
    row = lax.broadcasted_iota(jnp.int32, shape, 0)
    channel = lax.broadcasted_iota(jnp.int32, shape, 1) + chan * width
    wanted = jnp.zeros(shape, jnp.int32)
    for s in range(NSRC):
        wanted = jnp.where(row % NSRC == s, sources_ref[s], wanted)
    total = 0.0
    for w in range(count):
        pick = ((channel == wanted) & (row // NSRC == w)).astype(jnp.float32).astype(jnp.bfloat16)
        total = total + lax.dot_general(
            pick, spectra_ref[w], (((1,), (1,)), ((), ())), preferred_element_type=jnp.float32
        )
    return total.astype(jnp.bfloat16)


def correlate(x_ref, source_rows, inverse_ref, analytic, first_slot):
    pairs, depth, width = x_ref.shape
    bins, half = depth // 2, width // 2
    wide = NSRC * width
    shape = (source_rows.shape[0], wide)
    rows = lax.broadcasted_iota(jnp.int32, shape, 0)
    lane = lax.broadcasted_iota(jnp.int32, shape, 1)
    for pair in range(pairs):
        wanted = (2 * pair + lane % width // half) * NSRC + lane // width
        pick = (rows == wanted).astype(jnp.float32).astype(jnp.bfloat16)
        source = lax.dot_general(
            source_rows, pick, (((0,), (0,)), ((), ())), preferred_element_type=jnp.float32
        )
        channel = x_ref[pair].astype(jnp.float32)
        channel = jnp.concatenate([channel] * NSRC, 1)
        real_s, imag_s = source[:bins], source[bins:]
        real_x, imag_x = channel[:bins], channel[bins:]
        product = jnp.concatenate(
            [real_s * real_x + imag_s * imag_x, real_s * imag_x - imag_s * real_x], 0
        ).astype(jnp.bfloat16)
        analytic[first_slot + pair] = jnp.dot(
            inverse_ref[...], product, preferred_element_type=jnp.float32
        )


def stacks(analytic, weighted, forward_ref, spectrum, windows):
    slots, depth, wide = analytic.shape
    lags, width = depth // 2, wide // NSRC
    half = width // 2
    block = 16

    def stack(step, carry):
        start = pl.multiple_of(step * block, block)
        linear = phase_re = phase_im = 0.0
        for slot in range(slots):
            corr = analytic[slot, pl.ds(start, block)]
            hilb = analytic[slot, pl.ds(lags + start, block)]
            over = jnp.minimum(lax.rsqrt(corr * corr + hilb * hilb), 2.0)
            linear = linear + corr
            phase_re = phase_re + corr * over
            phase_im = phase_im + hilb * over

        def fold(value):
            parts = []
            for s in range(NSRC):
                part = value[:, s * width : (s + 1) * width]
                parts.append(part + pltpu.roll(part, half, 1))
            side = lax.broadcasted_iota(jnp.int32, (block, width), 1) < half
            return jnp.where(side, parts[0], parts[1])

        linear, phase_re, phase_im = fold(linear), fold(phase_re), fold(phase_im)
        result = linear * (phase_re * phase_re + phase_im * phase_im) * (1.0 / windows**3)
        weighted[pl.ds(start, block)] = result.astype(jnp.bfloat16)
        return carry

    lax.fori_loop(0, lags // block, stack, 0)
    result = lax.dot_general(
        weighted[...], forward_ref[...], (((0,), (0,)), ((), ())), preferred_element_type=jnp.float32
    )
    for part in range(lags // LANES):
        spectrum[part] = result[:, part * LANES : (part + 1) * LANES]


def slant(offset_ref, spectrum, base, sums, half, bins, scaling, part):
    sums[part] = jnp.zeros(sums.shape[1:], jnp.float32)
    steps = NSLOW // TILE
    low = lax.broadcasted_iota(jnp.int32, (TILE, LANES), 0)
    freq = lax.broadcasted_iota(jnp.int32, (TILE, LANES), 1) + part * LANES
    product = low * freq
    part_im = bins // LANES + part

    def group(number, carry):
        now, before, twice = [], [], []
        for member in range(GROUP):
            channel = number * GROUP + member
            offset = offset_ref[base + channel]
            jump_cos, jump_sin = cos_sin(freq * (offset * TILE))
            cosine, sine = cos_sin(product * offset)
            back_cos = cosine * jump_cos + sine * jump_sin
            back_sin = sine * jump_cos - cosine * jump_sin
            twice.append(2.0 * jump_cos)
            for s in range(NSRC):
                row = pl.ds(s * half + channel, 1)
                real = spectrum[part, row] * scaling
                imag = spectrum[part_im, row] * scaling
                now.append([real * cosine - imag * sine, real * sine + imag * cosine])
                before.append([real * back_cos - imag * back_sin, real * back_sin + imag * back_cos])
        for step in range(steps):
            for s in range(NSRC):
                for piece in range(2):
                    total = now[s][piece]
                    for member in range(1, GROUP):
                        total = total + now[member * NSRC + s][piece]
                    here = (part, s, piece, pl.ds(step * TILE, TILE))
                    sums[here] = sums[here] + total
            if step + 1 < steps:
                for member in range(GROUP):
                    for s in range(NSRC):
                        at = member * NSRC + s
                        for piece in range(2):
                            later = twice[member] * now[at][piece] - before[at][piece]
                            before[at][piece] = now[at][piece]
                            now[at][piece] = later
        return carry

    lax.fori_loop(0, half // GROUP, group, 0)


def kernel(
    windows, scaling, days, chans, spectra_ref, sources_ref, offset_ref, inverse_hbm, forward_hbm, out_ref,
    kept, sent, got, column, columns_far, plane, columns_near, analytic, weighted, spectrum, sums,
    leaving, arriving, owned, landing, inverse_ref, forward_ref, table_sem,
    half_sem, far_sem, near_sem, leave_sem, own_sem,
):
    count, depth, width = spectra_ref.shape
    bins, half = depth // 2, width // 2
    parts = bins // LANES
    far = chans // NEAR
    rows = NSLOW // chans
    day, chan = lax.axis_index("days"), lax.axis_index("chan")
    high, low = chan // NEAR, chan % NEAR
    table_copies = [
        pltpu.make_async_copy(inverse_hbm, inverse_ref, table_sem.at[0]),
        pltpu.make_async_copy(forward_hbm, forward_ref, table_sem.at[1]),
    ]
    for copy in table_copies:
        copy.start()

    near_peers = [
        (dd, dl, (day + dd) % days, (low + dl) % NEAR)
        for dd in range(days)
        for dl in range(NEAR)
        if dd or dl
    ]
    far_peers = [
        (dd, dh, (day + dd) % days, (high + dh) % far)
        for dd in range(days)
        for dh in range(far)
        if dd or dh
    ]
    barrier = pltpu.get_barrier_semaphore()
    greeted = 0
    for dd, dl, to_day, to_low in near_peers:
        pl.semaphore_signal(
            barrier, inc=1, device_id={"days": to_day, "chan": high * NEAR + to_low},
            device_id_type=pl.DeviceIdType.MESH,
        )
        greeted += 1
    for dd, dh, to_day, to_high in far_peers:
        if dh:
            pl.semaphore_signal(
                barrier, inc=1, device_id={"days": to_day, "chan": to_high * NEAR + low},
                device_id_type=pl.DeviceIdType.MESH,
            )
            greeted += 1
    column[...] = source_columns(spectra_ref, sources_ref, chan)
    pack_halves(spectra_ref, kept, sent, day)
    pl.semaphore_wait(barrier, greeted)

    far_copies = []
    for dd, dh, to_day, to_high in far_peers:
        if dd == 0:
            copy = exchange(
                column, columns_far.at[dh - 1], far_sem.at[0, dh - 1], far_sem.at[1, dh - 1],
                day, to_high * NEAR + low,
            )
            copy.start()
            far_copies.append(copy)
    half_copy = exchange(sent, got, half_sem.at[0], half_sem.at[1], (day + 1) % days, chan)
    half_copy.start()
    total = column[...].astype(jnp.float32)
    for index, copy in enumerate(far_copies):
        copy.wait_recv()
        total = total + columns_far[index].astype(jnp.float32)
    plane[...] = total.astype(jnp.bfloat16)
    near_copies = []
    for index, (dd, dl, to_day, to_low) in enumerate(near_peers):
        copy = exchange(
            plane, columns_near.at[index], near_sem.at[0, index], near_sem.at[1, index],
            to_day, high * NEAR + to_low,
        )
        copy.start()
        near_copies.append((dd, copy))

    def gather(wanted, value):
        for index, (dd, copy) in enumerate(near_copies):
            if dd == wanted:
                copy.wait_recv()
                value = value + columns_near[index].astype(jnp.float32)
        return value.astype(jnp.bfloat16)

    pairs = count // 2
    rows_own = gather(0, total)
    for copy in table_copies:
        copy.wait()
    correlate(kept, rows_own, inverse_ref, analytic, 0)
    rows_other = gather(1, 0.0)
    half_copy.wait_recv()
    correlate(got, rows_other, inverse_ref, analytic, pairs)
    stacks(analytic, weighted, forward_ref, spectrum, windows)

    leave_copies = []
    wire = leaving.dtype
    for part in range(parts):
        slant(offset_ref, spectrum, day * half, sums, half, bins, scaling, part)
        for lo in range(NEAR):
            for s in range(NSRC):
                for hi in range(far):
                    first = (hi * NEAR + lo) * rows
                    leaving[part, lo, s, :, hi * rows : (hi + 1) * rows] = sums[
                        part, s, :, first : first + rows
                    ].astype(wire)
        for index, (dd, dl, to_day, to_low) in enumerate(near_peers):
            copy = exchange(
                leaving.at[part, to_low, to_day], arriving.at[part, index],
                leave_sem.at[0, part, index], leave_sem.at[1, part, index],
                to_day, high * NEAR + to_low,
            )
            copy.start()
            leave_copies.append((part, index, copy))
    for part in range(parts):
        total = leaving[part, low, day].astype(jnp.float32)
        for at, index, copy in leave_copies:
            if at == part:
                copy.wait_recv()
                total = total + arriving[part, index].astype(jnp.float32)
        for hi in range(far):
            owned[hi, part] = total[:, hi * rows : (hi + 1) * rows].astype(wire)
    own_copies = []
    for index, (dd, dh, to_day, to_high) in enumerate(far_peers):
        copy = exchange(
            owned.at[to_high], landing.at[index], own_sem.at[0, index], own_sem.at[1, index],
            to_day, to_high * NEAR + low,
        )
        copy.start()
        own_copies.append((dd, index, copy))
    for shift in range(days):
        total = owned[high].astype(jnp.float32) if shift == 0 else 0.0
        for dd, index, copy in own_copies:
            if dd == shift:
                copy.wait_recv()
                total = total + landing[index].astype(jnp.float32)
        for part in range(parts):
            out_ref[(day + shift) % days, :, :, part * LANES : (part + 1) * LANES] = total[part]
    half_copy.wait_send()
    for copy in far_copies:
        copy.wait_send()
    for dd, copy in near_copies:
        copy.wait_send()
    for part, index, copy in leave_copies:
        copy.wait_send()
    for dd, index, copy in own_copies:
        copy.wait_send()


def shards(spectra, sources, offsets):
    count, depth, width = spectra.shape
    bins, half = depth // 2, width // 2
    days, chans = lax.axis_size("days"), lax.axis_size("chan")
    windows = count * days
    inverse, forward = tables(bins)
    scaling = windows**1.5 / math.sqrt(width * chans)
    far, rows, parts, pairs = chans // NEAR, NSLOW // chans, bins // LANES, count // 2
    near_count, far_count = days * NEAR - 1, days * far - 1
    wire = jnp.bfloat16 if rows % TILE == 0 else jnp.float32
    vmem = pl.BlockSpec(memory_space=pltpu.VMEM)
    smem = pl.BlockSpec(memory_space=pltpu.SMEM)
    anywhere = pl.BlockSpec(memory_space=pl.ANY)
    bf16, f32 = jnp.bfloat16, jnp.float32
    dma = pltpu.SemaphoreType.DMA
    out = pl.pallas_call(
        functools.partial(kernel, windows, scaling, days, chans),
        out_shape=jax.ShapeDtypeStruct((NSRC, 2, rows, bins), f32),
        in_specs=[vmem, smem, smem, anywhere, anywhere],
        out_specs=vmem,
        scratch_shapes=[
            pltpu.VMEM((pairs, depth, width), bf16),
            pltpu.VMEM((pairs, depth, width), bf16),
            pltpu.VMEM((pairs, depth, width), bf16),
            pltpu.VMEM((count * NSRC, depth), bf16),
            pltpu.VMEM((far - 1, count * NSRC, depth), bf16),
            pltpu.VMEM((count * NSRC, depth), bf16),
            pltpu.VMEM((near_count, count * NSRC, depth), bf16),
            pltpu.VMEM((2 * pairs, 2 * depth, NSRC * width), f32),
            pltpu.VMEM((depth, width), bf16),
            pltpu.VMEM((depth // LANES, NSRC * half, LANES), f32),
            pltpu.VMEM((parts, NSRC, 2, NSLOW, LANES), f32),
            pltpu.VMEM((parts, NEAR, NSRC, 2, far * rows, LANES), wire),
            pltpu.VMEM((parts, near_count, 2, far * rows, LANES), wire),
            pltpu.VMEM((far, parts, 2, rows, LANES), wire),
            pltpu.VMEM((far_count, parts, 2, rows, LANES), wire),
            pltpu.VMEM(inverse.shape, bf16),
            pltpu.VMEM(forward.shape, bf16),
            dma((2,)),
            dma((2,)),
            dma((2, far - 1)),
            dma((2, near_count)),
            dma((2, parts, near_count)),
            dma((2, far_count)),
        ],
        compiler_params=pltpu.CompilerParams(collective_id=0, has_side_effects=True),
    )(spectra, sources, offsets, jnp.asarray(inverse), jnp.asarray(forward))
    return out.transpose(2, 0, 1, 3)


def solution(mesh):
    placed = (P("days", None, "chan"), P(), P("chan"))
    return jax.shard_map(
        shards, mesh=mesh, in_specs=placed, out_specs=P("chan", None, None, None), check_vma=False
    )
```

time: 142 us -> 36.7 us (0.26)
  waiting for transfers between devices: 55.1 us -> 0 us
  blocking collectives: 42.7 us -> 0 us
  Pallas kernels: 14 us -> 35.1 us
  between operations: 19.8 us -> 0.01 us
  starting transfers between devices: 3.96 us -> 0 us
  local copies, waits for them, and re-layouts: 5.03 us -> 1.39 us
    reduce_scatter x1 -> x0, waiting for transfers between devices: 52.9 us -> none  [shards(): lax.psum_scatter(partial.transpose(2, 0, 1, 3), 'chan', scatter_dimension...]
    psum x2 -> x0, blocking collectives: 42.7 us -> none  [the longest x1 33.7 us: shards(): own = lax.psum(jnp.stack(collected, 1), 'chan')]
    pallas_call x1, Pallas kernels: 14 us -> 35.1 us  [shards(): pl.pallas_call(functools.partial(kernel, windows, scaling, days, chans),...]
    ppermute x2 -> x0, starting transfers between devices: 3.96 us -> none  [the longest x1 3.03 us: shards(): got = lax.ppermute(sent, 'days', swap)]
    dynamic_slice x3 -> x0, local copies, waits for them, and re-layouts: 2.55 us -> none  [the longest x1 1.61 us: shards(): kept = lax.dynamic_slice_in_dim(spectra, me * half, half, 2)]
    ppermute x2 -> x0, waiting for transfers between devices: 2.21 us -> none  [the longest x1 2.21 us: shards(): other = lax.ppermute(own, 'days', swap)]
  transfers between devices with their start and end apart: 3 -> 0, of which waited for: 2 -> 0; matrix products, arithmetic and copies ran while one was open for 2% -> 0% of each run, Pallas kernels for 0% -> 0%
where the time goes in v2:
time: 36.7 us; the launch traced here: 36.5 us
  Pallas kernels  35.1 us (96%)
  local copies, waits for them, and re-layouts  1.39 us (4%)
    pallas_call x1, Pallas kernels, shards(): pl.pallas_call(functools.partial(kernel, windows, scaling, days, chans),...  35.1 us
    transpose x1, local copies, waits for them, and re-layouts, shards(): return out.transpose(2, 0, 1, 3)  1.39 us

profile of v2, /device:TPU:0, one launch (start us, length us, event | category | flops | bytes accessed | tf_op | source)
XLA Modules:
  0.0 36.5 jit_solution(211593618738889811)
XLA Ops:
  0.0 35.1 %shard_map.55 = f32[2,2,8,256]{3,2,1,0:T(8,128)} custom-call(bf16[4,512,128]{2,1,0:T(8,128)(2,1)} %spectra_ref.1, s32[2]{0:T(128)} %sources_ref.1, s32[128]{0:T(128)} %offset_ref.1, bf16[1024,512]{1,0:T(8,128)(2,1)} %constant.4.clone.inverse_hbm, bf16[512,512]{1,0:T(8,128)(2,1)} %constant.5.clone.forward_hbm), custom_call_target="tpu_custom_call" | custom-call | tf_op jit(solution)/shard_map/pallas_call | solution.py:365
  35.1 1.4 %copy.6 = f32[8,2,2,256]{3,2,1,0:T(2,128)} copy(f32[8,2,2,256]{3,0,2,1:T(8,128)} %bitcast.1) | data formatting | bytes 65536 | tf_op jit(solution)/shard_map/transpose | solution.py:397

commit v3 on v2

--- a/solution.py
+++ b/solution.py
@@ -117,7 +117,7 @@
         )
 
 
-def stacks(analytic, weighted, forward_ref, spectrum, windows):
+def stacks(analytic, weighted, forward_ref, spectrum, factor):
     slots, depth, wide = analytic.shape
     lags, width = depth // 2, wide // NSRC
     half = width // 2
@@ -143,11 +143,11 @@
             return jnp.where(side, parts[0], parts[1])
 
         linear, phase_re, phase_im = fold(linear), fold(phase_re), fold(phase_im)
-        result = linear * (phase_re * phase_re + phase_im * phase_im) * (1.0 / windows**3)
+        result = linear * (phase_re * phase_re + phase_im * phase_im) * factor
         weighted[pl.ds(start, block)] = result.astype(jnp.bfloat16)
         return carry
 
-    lax.fori_loop(0, lags // block, stack, 0)
+    lax.fori_loop(0, lags // block, stack, 0, unroll=4)
     result = lax.dot_general(
         weighted[...], forward_ref[...], (((0,), (0,)), ((), ())), preferred_element_type=jnp.float32
     )
@@ -155,28 +155,42 @@
         spectrum[part] = result[:, part * LANES : (part + 1) * LANES]
 
 
-def slant(offset_ref, spectrum, base, sums, half, bins, scaling, part):
-    sums[part] = jnp.zeros(sums.shape[1:], jnp.float32)
-    steps = NSLOW // TILE
+def phase_tables(offset_ref, base, phases, half, part):
     low = lax.broadcasted_iota(jnp.int32, (TILE, LANES), 0)
     freq = lax.broadcasted_iota(jnp.int32, (TILE, LANES), 1) + part * LANES
     product = low * freq
-    part_im = bins // LANES + part
 
     def group(number, carry):
-        now, before, twice = [], [], []
         for member in range(GROUP):
             channel = number * GROUP + member
             offset = offset_ref[base + channel]
             jump_cos, jump_sin = cos_sin(freq * (offset * TILE))
             cosine, sine = cos_sin(product * offset)
-            back_cos = cosine * jump_cos + sine * jump_sin
-            back_sin = sine * jump_cos - cosine * jump_sin
-            twice.append(2.0 * jump_cos)
+            phases[part, channel, 0] = cosine
+            phases[part, channel, 1] = sine
+            phases[part, channel, 2] = cosine * jump_cos + sine * jump_sin
+            phases[part, channel, 3] = sine * jump_cos - cosine * jump_sin
+            phases[part, channel, 4] = 2.0 * jump_cos
+        return carry
+
+    lax.fori_loop(0, half // GROUP, group, 0)
+
+
+def slant(phases, spectrum, sums, half, bins, part):
+    sums[part] = jnp.zeros(sums.shape[1:], jnp.float32)
+    steps = NSLOW // TILE
+    part_im = bins // LANES + part
+
+    def group(number, carry):
+        now, before, twice = [], [], []
+        for member in range(GROUP):
+            channel = number * GROUP + member
+            cosine, sine = phases[part, channel, 0], phases[part, channel, 1]
+            back_cos, back_sin = phases[part, channel, 2], phases[part, channel, 3]
+            twice.append(phases[part, channel, 4])
             for s in range(NSRC):
                 row = pl.ds(s * half + channel, 1)
-                real = spectrum[part, row] * scaling
-                imag = spectrum[part_im, row] * scaling
+                real, imag = spectrum[part, row], spectrum[part_im, row]
                 now.append([real * cosine - imag * sine, real * sine + imag * cosine])
                 before.append([real * back_cos - imag * back_sin, real * back_sin + imag * back_cos])
         for step in range(steps):
@@ -202,7 +216,7 @@
 
 def kernel(
     windows, scaling, days, chans, spectra_ref, sources_ref, offset_ref, inverse_hbm, forward_hbm, out_ref,
-    kept, sent, got, column, columns_far, plane, columns_near, analytic, weighted, spectrum, sums,
+    kept, sent, got, column, columns_far, plane, columns_near, analytic, weighted, spectrum, sums, phases,
     leaving, arriving, owned, landing, inverse_ref, forward_ref, table_sem,
     half_sem, far_sem, near_sem, leave_sem, own_sem,
 ):
@@ -262,6 +276,7 @@
             far_copies.append(copy)
     half_copy = exchange(sent, got, half_sem.at[0], half_sem.at[1], (day + 1) % days, chan)
     half_copy.start()
+    phase_tables(offset_ref, day * half, phases, half, 0)
     total = column[...].astype(jnp.float32)
     for index, copy in enumerate(far_copies):
         copy.wait_recv()
@@ -275,6 +290,8 @@
         )
         copy.start()
         near_copies.append((dd, copy))
+    for part in range(1, parts):
+        phase_tables(offset_ref, day * half, phases, half, part)
 
     def gather(wanted, value):
         for index, (dd, copy) in enumerate(near_copies):
@@ -291,12 +308,12 @@
     rows_other = gather(1, 0.0)
     half_copy.wait_recv()
     correlate(got, rows_other, inverse_ref, analytic, pairs)
-    stacks(analytic, weighted, forward_ref, spectrum, windows)
+    stacks(analytic, weighted, forward_ref, spectrum, scaling / windows**3)
 
     leave_copies = []
     wire = leaving.dtype
     for part in range(parts):
-        slant(offset_ref, spectrum, day * half, sums, half, bins, scaling, part)
+        slant(phases, spectrum, sums, half, bins, part)
         for lo in range(NEAR):
             for s in range(NSRC):
                 for hi in range(far):
@@ -335,7 +352,8 @@
                 copy.wait_recv()
                 total = total + landing[index].astype(jnp.float32)
         for part in range(parts):
-            out_ref[(day + shift) % days, :, :, part * LANES : (part + 1) * LANES] = total[part]
+            for piece in range(2):
+                out_ref[:, (day + shift) % days, piece, part * LANES : (part + 1) * LANES] = total[part, piece]
     half_copy.wait_send()
     for copy in far_copies:
         copy.wait_send()
@@ -362,9 +380,9 @@
     anywhere = pl.BlockSpec(memory_space=pl.ANY)
     bf16, f32 = jnp.bfloat16, jnp.float32
     dma = pltpu.SemaphoreType.DMA
-    out = pl.pallas_call(
+    return pl.pallas_call(
         functools.partial(kernel, windows, scaling, days, chans),
-        out_shape=jax.ShapeDtypeStruct((NSRC, 2, rows, bins), f32),
+        out_shape=jax.ShapeDtypeStruct((rows, NSRC, 2, bins), f32),
         in_specs=[vmem, smem, smem, anywhere, anywhere],
         out_specs=vmem,
         scratch_shapes=[
@@ -379,6 +397,7 @@
             pltpu.VMEM((depth, width), bf16),
             pltpu.VMEM((depth // LANES, NSRC * half, LANES), f32),
             pltpu.VMEM((parts, NSRC, 2, NSLOW, LANES), f32),
+            pltpu.VMEM((parts, half, 5, TILE, LANES), f32),
             pltpu.VMEM((parts, NEAR, NSRC, 2, far * rows, LANES), wire),
             pltpu.VMEM((parts, near_count, 2, far * rows, LANES), wire),
             pltpu.VMEM((far, parts, 2, rows, LANES), wire),
@@ -394,7 +413,6 @@
         ],
         compiler_params=pltpu.CompilerParams(collective_id=0, has_side_effects=True),
     )(spectra, sources, offsets, jnp.asarray(inverse), jnp.asarray(forward))
-    return out.transpose(2, 0, 1, 3)
 
 
 def solution(mesh):

time: 36.7 us -> 32.4 us (0.88)
  Pallas kernels: 35.1 us -> 30.9 us
    pallas_call x1, Pallas kernels: 35.1 us -> 30.9 us  [shards(): pl.pallas_call(functools.partial(kernel, windows, scaling, days, chans),...]
    transpose x1 -> x0, local copies, waits for them, and re-layouts: 1.39 us -> none  [shards(): return out.transpose(2, 0, 1, 3)]
    unnamed x0 -> x1, local copies, waits for them, and re-layouts: none -> 1.38 us
where the time goes in v3:
time: 32.4 us; the launch traced here: 32.2 us
  Pallas kernels  30.9 us (95%)
  local copies, waits for them, and re-layouts  1.38 us (4%)
    pallas_call x1, Pallas kernels, shards(): pl.pallas_call(functools.partial(kernel, windows, scaling, days, chans),...  30.9 us
    unnamed x1, local copies, waits for them, and re-layouts  1.38 us

profile of v3, /device:TPU:0, one launch (start us, length us, event | category | flops | bytes accessed | tf_op | source)
XLA Modules:
  0.0 32.2 jit_solution(9461851027315902536)
XLA Ops:
  0.0 30.9 %shard_map.55 = f32[8,2,2,256]{3,2,1,0:T(2,128)} custom-call(bf16[4,512,128]{2,1,0:T(8,128)(2,1)} %spectra_ref.1, s32[2]{0:T(128)} %sources_ref.1, s32[128]{0:T(128)} %offset_ref.1, bf16[1024,512]{1,0:T(8,128)(2,1)} %constant.4.clone.inverse_hbm, bf16[512,512]{1,0:T(8,128)(2,1)} %constant.5.clone.forward_hbm), custom_call_target="tpu_custom_call" | custom-call | tf_op jit(solution)/shard_map/pallas_call | solution.py:383
  30.9 1.4 %copy.7 = f32[8,2,2,256]{3,2,1,0:T(2,128)} copy(f32[8,2,2,256]{3,2,1,0:T(2,128)} %shard_map.55) | data formatting | bytes 65536

commit v4 on v3

--- a/solution.py
+++ b/solution.py
@@ -15,6 +15,7 @@
 TILE = 8
 LANES = 128
 GROUP = 2
+SLANT_GROUP = 4
 NEAR = 4
 
 
@@ -117,22 +118,41 @@
         )
 
 
-def stacks(analytic, weighted, forward_ref, spectrum, factor):
-    slots, depth, wide = analytic.shape
-    lags, width = depth // 2, wide // NSRC
+def stack_sums(analytic, slots, start, block, lags, totals):
+    linear, phase_re, phase_im = totals
+    for slot in slots:
+        corr = analytic[slot, pl.ds(start, block)]
+        hilb = analytic[slot, pl.ds(lags + start, block)]
+        over = jnp.minimum(lax.rsqrt(corr * corr + hilb * hilb), 2.0)
+        linear = linear + corr
+        phase_re = phase_re + corr * over
+        phase_im = phase_im + hilb * over
+    return linear, phase_re, phase_im
+
+
+def first_stacks(analytic, slots, held):
+    lags = analytic.shape[1] // 2
+    block = 16
+
+    def stack(step, carry):
+        start = pl.multiple_of(step * block, block)
+        totals = stack_sums(analytic, slots, start, block, lags, (0.0, 0.0, 0.0))
+        for index, total in enumerate(totals):
+            held[index, pl.ds(start, block)] = total
+        return carry
+
+    lax.fori_loop(0, lags // block, stack, 0, unroll=4)
+
+
+def last_stacks(analytic, slots, held, weighted, forward_ref, spectrum, factor):
+    lags, width = analytic.shape[1] // 2, analytic.shape[2] // NSRC
     half = width // 2
     block = 16
 
     def stack(step, carry):
         start = pl.multiple_of(step * block, block)
-        linear = phase_re = phase_im = 0.0
-        for slot in range(slots):
-            corr = analytic[slot, pl.ds(start, block)]
-            hilb = analytic[slot, pl.ds(lags + start, block)]
-            over = jnp.minimum(lax.rsqrt(corr * corr + hilb * hilb), 2.0)
-            linear = linear + corr
-            phase_re = phase_re + corr * over
-            phase_im = phase_im + hilb * over
+        totals = tuple(held[index, pl.ds(start, block)] for index in range(3))
+        totals = stack_sums(analytic, slots, start, block, lags, totals)
 
         def fold(value):
             parts = []
@@ -142,7 +162,7 @@
             side = lax.broadcasted_iota(jnp.int32, (block, width), 1) < half
             return jnp.where(side, parts[0], parts[1])
 
-        linear, phase_re, phase_im = fold(linear), fold(phase_re), fold(phase_im)
+        linear, phase_re, phase_im = (fold(total) for total in totals)
         result = linear * (phase_re * phase_re + phase_im * phase_im) * factor
         weighted[pl.ds(start, block)] = result.astype(jnp.bfloat16)
         return carry
@@ -176,47 +196,43 @@
     lax.fori_loop(0, half // GROUP, group, 0)
 
 
-def slant(phases, spectrum, sums, half, bins, part):
-    sums[part] = jnp.zeros(sums.shape[1:], jnp.float32)
+def slant(phases, spectrum, sums, half, bins, part, source):
+    sums[part, source] = jnp.zeros(sums.shape[2:], jnp.float32)
     steps = NSLOW // TILE
     part_im = bins // LANES + part
 
     def group(number, carry):
         now, before, twice = [], [], []
-        for member in range(GROUP):
-            channel = number * GROUP + member
+        for member in range(SLANT_GROUP):
+            channel = number * SLANT_GROUP + member
             cosine, sine = phases[part, channel, 0], phases[part, channel, 1]
             back_cos, back_sin = phases[part, channel, 2], phases[part, channel, 3]
             twice.append(phases[part, channel, 4])
-            for s in range(NSRC):
-                row = pl.ds(s * half + channel, 1)
-                real, imag = spectrum[part, row], spectrum[part_im, row]
-                now.append([real * cosine - imag * sine, real * sine + imag * cosine])
-                before.append([real * back_cos - imag * back_sin, real * back_sin + imag * back_cos])
+            row = pl.ds(source * half + channel, 1)
+            real, imag = spectrum[part, row], spectrum[part_im, row]
+            now.append([real * cosine - imag * sine, real * sine + imag * cosine])
+            before.append([real * back_cos - imag * back_sin, real * back_sin + imag * back_cos])
         for step in range(steps):
-            for s in range(NSRC):
-                for piece in range(2):
-                    total = now[s][piece]
-                    for member in range(1, GROUP):
-                        total = total + now[member * NSRC + s][piece]
-                    here = (part, s, piece, pl.ds(step * TILE, TILE))
-                    sums[here] = sums[here] + total
+            for piece in range(2):
+                total = now[0][piece]
+                for member in range(1, SLANT_GROUP):
+                    total = total + now[member][piece]
+                here = (part, source, piece, pl.ds(step * TILE, TILE))
+                sums[here] = sums[here] + total
             if step + 1 < steps:
-                for member in range(GROUP):
-                    for s in range(NSRC):
-                        at = member * NSRC + s
-                        for piece in range(2):
-                            later = twice[member] * now[at][piece] - before[at][piece]
-                            before[at][piece] = now[at][piece]
-                            now[at][piece] = later
+                for member in range(SLANT_GROUP):
+                    for piece in range(2):
+                        later = twice[member] * now[member][piece] - before[member][piece]
+                        before[member][piece] = now[member][piece]
+                        now[member][piece] = later
         return carry
 
-    lax.fori_loop(0, half // GROUP, group, 0)
+    lax.fori_loop(0, half // SLANT_GROUP, group, 0)
 
 
 def kernel(
-    windows, scaling, days, chans, spectra_ref, sources_ref, offset_ref, inverse_hbm, forward_hbm, out_ref,
-    kept, sent, got, column, columns_far, plane, columns_near, analytic, weighted, spectrum, sums, phases,
+    windows, scaling, days, chans, spectra_hbm, sources_ref, offset_ref, inverse_hbm, forward_hbm, out_ref,
+    kept, sent, got, column, columns_far, plane, columns_near, analytic, weighted, spectrum, sums, phases, held, spectra_ref,
     leaving, arriving, owned, landing, inverse_ref, forward_ref, table_sem,
     half_sem, far_sem, near_sem, leave_sem, own_sem,
 ):
@@ -231,9 +247,6 @@
         pltpu.make_async_copy(inverse_hbm, inverse_ref, table_sem.at[0]),
         pltpu.make_async_copy(forward_hbm, forward_ref, table_sem.at[1]),
     ]
-    for copy in table_copies:
-        copy.start()
-
     near_peers = [
         (dd, dl, (day + dd) % days, (low + dl) % NEAR)
         for dd in range(days)
@@ -261,6 +274,11 @@
                 device_id_type=pl.DeviceIdType.MESH,
             )
             greeted += 1
+    spectra_copy = pltpu.make_async_copy(spectra_hbm, spectra_ref, table_sem.at[2])
+    spectra_copy.start()
+    for copy in table_copies:
+        copy.start()
+    spectra_copy.wait()
     column[...] = source_columns(spectra_ref, sources_ref, chan)
     pack_halves(spectra_ref, kept, sent, day)
     pl.semaphore_wait(barrier, greeted)
@@ -305,30 +323,35 @@
     for copy in table_copies:
         copy.wait()
     correlate(kept, rows_own, inverse_ref, analytic, 0)
+    first_stacks(analytic, range(pairs), held)
     rows_other = gather(1, 0.0)
     half_copy.wait_recv()
     correlate(got, rows_other, inverse_ref, analytic, pairs)
-    stacks(analytic, weighted, forward_ref, spectrum, scaling / windows**3)
+    others = range(pairs, 2 * pairs)
+    last_stacks(analytic, others, held, weighted, forward_ref, spectrum, scaling / windows**3)
 
     leave_copies = []
     wire = leaving.dtype
-    for part in range(parts):
-        slant(phases, spectrum, sums, half, bins, part)
-        for lo in range(NEAR):
-            for s in range(NSRC):
+    for turn in range(days):
+        shift = days - 1 - turn
+        target = (day + shift) % days
+        for part in range(parts):
+            slant(phases, spectrum, sums, half, bins, part, target)
+            for lo in range(NEAR):
                 for hi in range(far):
                     first = (hi * NEAR + lo) * rows
-                    leaving[part, lo, s, :, hi * rows : (hi + 1) * rows] = sums[
-                        part, s, :, first : first + rows
+                    leaving[part, lo, target, :, hi * rows : (hi + 1) * rows] = sums[
+                        part, target, :, first : first + rows
                     ].astype(wire)
-        for index, (dd, dl, to_day, to_low) in enumerate(near_peers):
-            copy = exchange(
-                leaving.at[part, to_low, to_day], arriving.at[part, index],
-                leave_sem.at[0, part, index], leave_sem.at[1, part, index],
-                to_day, high * NEAR + to_low,
-            )
-            copy.start()
-            leave_copies.append((part, index, copy))
+            for index, (dd, dl, to_day, to_low) in enumerate(near_peers):
+                if dd == shift:
+                    copy = exchange(
+                        leaving.at[part, to_low, target], arriving.at[part, index],
+                        leave_sem.at[0, part, index], leave_sem.at[1, part, index],
+                        target, high * NEAR + to_low,
+                    )
+                    copy.start()
+                    leave_copies.append((part, index, copy))
     for part in range(parts):
         total = leaving[part, low, day].astype(jnp.float32)
         for at, index, copy in leave_copies:
@@ -383,7 +406,7 @@
     return pl.pallas_call(
         functools.partial(kernel, windows, scaling, days, chans),
         out_shape=jax.ShapeDtypeStruct((rows, NSRC, 2, bins), f32),
-        in_specs=[vmem, smem, smem, anywhere, anywhere],
+        in_specs=[anywhere, smem, smem, anywhere, anywhere],
         out_specs=vmem,
         scratch_shapes=[
             pltpu.VMEM((pairs, depth, width), bf16),
@@ -398,13 +421,15 @@
             pltpu.VMEM((depth // LANES, NSRC * half, LANES), f32),
             pltpu.VMEM((parts, NSRC, 2, NSLOW, LANES), f32),
             pltpu.VMEM((parts, half, 5, TILE, LANES), f32),
+            pltpu.VMEM((3, depth, NSRC * width), f32),
+            pltpu.VMEM((count, depth, width), bf16),
             pltpu.VMEM((parts, NEAR, NSRC, 2, far * rows, LANES), wire),
             pltpu.VMEM((parts, near_count, 2, far * rows, LANES), wire),
             pltpu.VMEM((far, parts, 2, rows, LANES), wire),
             pltpu.VMEM((far_count, parts, 2, rows, LANES), wire),
             pltpu.VMEM(inverse.shape, bf16),
             pltpu.VMEM(forward.shape, bf16),
-            dma((2,)),
+            dma((3,)),
             dma((2,)),
             dma((2, far - 1)),
             dma((2, near_count)),

time: 32.4 us -> 31.6 us (0.975)
  Pallas kernels: 30.9 us -> 30 us
    pallas_call x1, Pallas kernels: 30.9 us -> 30 us  [shards(): pl.pallas_call(functools.partial(kernel, windows, scaling, days, chans),...]
where the time goes in v4:
time: 31.6 us; the launch traced here: 31.4 us
  Pallas kernels  30 us (95%)
  local copies, waits for them, and re-layouts  1.38 us (4%)
    pallas_call x1, Pallas kernels, shards(): pl.pallas_call(functools.partial(kernel, windows, scaling, days, chans),...  30 us
    unnamed x1, local copies, waits for them, and re-layouts  1.38 us

profile of v4, /device:TPU:0, one launch (start us, length us, event | category | flops | bytes accessed | tf_op | source)
XLA Modules:
  0.0 31.4 jit_solution(7363868399974637696)
XLA Ops:
  0.0 30.0 %shard_map.55 = f32[8,2,2,256]{3,2,1,0:T(2,128)} custom-call(bf16[4,512,128]{2,1,0:T(8,128)(2,1)} %spectra_hbm.1, s32[2]{0:T(128)} %sources_ref.1, s32[128]{0:T(128)} %offset_ref.1, bf16[1024,512]{1,0:T(8,128)(2,1)} %constant.4.clone.inverse_hbm, bf16[512,512]{1,0:T(8,128)(2,1)} %constant.5.clone.forward_hbm), custom_call_target="tpu_custom_call" | custom-call | tf_op jit(solution)/shard_map/pallas_call | solution.py:406
  30.0 1.4 %copy.7 = f32[8,2,2,256]{3,2,1,0:T(2,128)} copy(f32[8,2,2,256]{3,2,1,0:T(2,128)} %shard_map.55) | data formatting | bytes 65536

commit v5 on v4

--- a/solution.py
+++ b/solution.py
@@ -376,7 +376,7 @@
                 total = total + landing[index].astype(jnp.float32)
         for part in range(parts):
             for piece in range(2):
-                out_ref[:, (day + shift) % days, piece, part * LANES : (part + 1) * LANES] = total[part, piece]
+                out_ref[:, (day + shift) % days, part, piece] = total[part, piece]
     half_copy.wait_send()
     for copy in far_copies:
         copy.wait_send()
@@ -403,9 +403,9 @@
     anywhere = pl.BlockSpec(memory_space=pl.ANY)
     bf16, f32 = jnp.bfloat16, jnp.float32
     dma = pltpu.SemaphoreType.DMA
-    return pl.pallas_call(
+    out = pl.pallas_call(
         functools.partial(kernel, windows, scaling, days, chans),
-        out_shape=jax.ShapeDtypeStruct((rows, NSRC, 2, bins), f32),
+        out_shape=jax.ShapeDtypeStruct((rows, NSRC, parts, 2, LANES), f32),
         in_specs=[anywhere, smem, smem, anywhere, anywhere],
         out_specs=vmem,
         scratch_shapes=[
@@ -438,6 +438,7 @@
         ],
         compiler_params=pltpu.CompilerParams(collective_id=0, has_side_effects=True),
     )(spectra, sources, offsets, jnp.asarray(inverse), jnp.asarray(forward))
+    return out.transpose(0, 1, 3, 2, 4).reshape(rows, NSRC, 2, bins)
 
 
 def solution(mesh):

time: 31.6 us -> 31.6 us (level)
  no operation moved by 1% of the time
where the time goes in v5:
time: 31.6 us; the launch traced here: 31.4 us
  Pallas kernels  30 us (95%)
  local copies, waits for them, and re-layouts  1.38 us (4%)
    pallas_call x1, Pallas kernels, shards(): pl.pallas_call(functools.partial(kernel, windows, scaling, days, chans),...  30 us
    unnamed x1, local copies, waits for them, and re-layouts  1.38 us

profile of v5, /device:TPU:0, one launch (start us, length us, event | category | flops | bytes accessed | tf_op | source)
XLA Modules:
  0.0 31.4 jit_solution(13098962985944296561)
XLA Ops:
  0.0 30.0 %shard_map.55 = f32[8,2,2,2,128]{4,3,2,1,0:T(2,128)} custom-call(bf16[4,512,128]{2,1,0:T(8,128)(2,1)} %spectra_hbm.1, s32[2]{0:T(128)} %sources_ref.1, s32[128]{0:T(128)} %offset_ref.1, bf16[1024,512]{1,0:T(8,128)(2,1)} %constant.4.clone.inverse_hbm, bf16[512,512]{1,0:T(8,128)(2,1)} %constant.5.clone.forward_hbm), custom_call_target="tpu_custom_call" | custom-call | tf_op jit(solution)/shard_map/pallas_call | solution.py:406
  30.0 1.4 %copy.7 = f32[8,2,2,256]{3,2,1,0:T(2,128)} copy(f32[8,2,2,256]{3,2,1,0:T(2,128)} %bitcast.3) | data formatting | bytes 65536
